TPU v7x, 512 devices: a whole 4x8x8 slice. The times are simulated.
512 devices in a mesh: row: 16 (over z, core), col: 32 (over x, y).
Axes of the slice: x: 4, y: 8, z: 8, core: 2. Of those that a mesh axis runs over, the one named last changes fastest.
Arguments:
- u_front: bfloat16 [2, 2048, 25, 2048], P(None, 'col', None, 'row'), may hold values from -0.02734375 to 0.02734375
- inverse_blocks: bfloat16 [2, 2048, 1, 2048], P(None, 'col', None, 'row')
- rhs_window: float32 [32, 2, 2048], P(None, None, 'col'), may hold values from -6 to 6
- pivot_inverse: float32 [2, 2048], P(None, 'col'), may hold values from 0.25 to 4
- below_solution: bfloat16 [32, 23, 2048], P(None, None, 'row'), may hold values from -6 to 6
- u_child: bfloat16 [4096, 16, 2048], P('col', None, 'row'), may hold values from -0.03125 to 0.03125
- rhs_child: float32 [32, 4096], P(None, 'col'), may hold values from -6 to 6
- child_map: int32 [2, 256], replicated, may hold values from 0 to 399, as said below
- child_counts: int32 [2], replicated, may hold values from 128 to 256, as said below
Outputs:
- x_window: float32 [32, 2, 2048], P(None, None, 'row')
- child_out: float32 [32, 4096], P(None, 'col')
Inputs may be any that keep to these rules, and one draw needn't show every extreme that they name: Slot s of a child lies on row index s % 16 of the child's rows, and the block it names lies on row index (s % 16 + s // 16) % 16 of the front's rows, that is child_map[h, s] % 16 equals that number; one child names each block at most once; both ends of the range are named. `child_counts`: one of the two children uses all 256 slots.
All inputs are finite; a program needn't handle non-finite values.
Results may differ from a plain program's by a relative error of at most 0.003.
Values may be sent and summed in bfloat16 or wider, within the bound.
A program may use at most 64 MiB of HBM per device.

v0:
```python
import jax
import jax.numpy as jnp
from jax import lax
from jax.sharding import PartitionSpec as P


def local(
    u_front,
    inverse_blocks,
    rhs_window,
    pivot_inverse,
    below_solution,
    u_child,
    rhs_child,
    child_map,
    child_counts,
):
    panel_count = u_front.shape[0]
    front_blocks = u_front.shape[2]
    block_rows = u_front.shape[3]
    panel_blocks = inverse_blocks.shape[2]
    window_blocks = panel_count * panel_blocks
    rhs_count = rhs_window.shape[0]
    scaled = rhs_window * pivot_inverse[None]
    solved = [None] * panel_count
    solved_rows = jnp.concatenate(
        [jnp.zeros((rhs_count, window_blocks, block_rows), jnp.bfloat16), below_solution], axis=1
    )
    for panel_index in reversed(range(panel_count)):
        partial_value = jnp.einsum(
            "wqb,nqb->nw", u_front[panel_index], solved_rows, preferred_element_type=jnp.float32
        )
        summed = lax.psum(partial_value, "row")
        reduced = (scaled[:, panel_index] - summed).astype(jnp.bfloat16)
        partial_share = jnp.einsum(
            "nw,wpb->npb", reduced, inverse_blocks[panel_index], preferred_element_type=jnp.float32
        )
        result = lax.psum(partial_share, "col")
        solved[panel_index] = result
        lower_edge = panel_index * panel_blocks
        solved_rows = lax.dynamic_update_slice_in_dim(
            solved_rows, result.astype(jnp.bfloat16), lower_edge, 1
        )
    x_window = jnp.concatenate(solved, axis=1)
    row_count = lax.axis_size("row")
    my_row = lax.axis_index("row")
    half_width = lax.axis_size("col") // 2
    which_child = lax.axis_index("col") // half_width
    slot_depth = u_child.shape[1]
    child_slots = child_map[which_child]
    local_slots = jnp.arange(slot_depth, dtype=jnp.int32) * row_count + my_row
    wanted = child_slots[local_slots]
    live_mask = (local_slots < child_counts[which_child]).astype(jnp.bfloat16)
    section = lax.all_gather(solved_rows, "row", axis=1, tiled=True)
    length = section.shape[1]
    gathered_index = jnp.arange(length, dtype=jnp.int32)
    global_block = gathered_index % front_blocks * row_count + gathered_index // front_blocks
    selector = (wanted[:, None] == global_block[None, :]).astype(jnp.bfloat16)
    incoming = jnp.einsum(
        "sq,nqb->nsb", selector, section, preferred_element_type=jnp.float32
    ).astype(jnp.bfloat16)
    masked = incoming * live_mask[None, :, None]
    child_part = jnp.einsum("psb,nsb->np", u_child, masked, preferred_element_type=jnp.float32)
    child_total = lax.psum(child_part, "row")
    child_out = rhs_child - child_total
    return (x_window, child_out)


def solution(mesh):
    return jax.shard_map(
        local,
        mesh=mesh,
        in_specs=(
            P(None, "col", None, "row"),
            P(None, "col", None, "row"),
            P(None, None, "col"),
            P(None, "col"),
            P(None, None, "row"),
            P("col", None, "row"),
            P(None, "col"),
            P(),
            P(),
        ),
        out_specs=(P(None, None, "row"), P(None, "col")),
        check_vma=False,
    )
```

profile of v0, /device:TPU:1, one launch (start us, length us, event | category | flops | bytes accessed | tf_op | source)
XLA Modules:
  0.0 483.7 jit_solution(11730641307680731013)
XLA Ops:
  7.2 0.0 copy-start
  7.2 0.0 all-gather.2.cloned.1.call-start
  7.2 1.4 convolution_bitcast_fusion.3
  8.6 52.0 %psum.35 = f32[32,64]{1,0:T(8,128)S(1)} all-reduce(f32[32,64]{1,0:T(8,128)S(1)} %convolution_bitcast_fusion.3), channel_id=1, replica_groups=mesh['row'=16,'col'=32] {'row'}, use_global_device_ids=true, to_apply=%region_0.0 | all-reduce | flops 2048 | bytes 16384 | tf_op jit(solution)/shard_map/psum | solution.py:33
  60.6 0.8 copy_multiply_fusion
  61.4 0.8 convolution_bitcast_fusion.2
  62.2 115.7 %psum.36 = f32[32,1,128]{2,0,1:T(8,128)S(1)} all-reduce(f32[32,1,128]{2,0,1:T(8,128)S(1)} %convolution_bitcast_fusion.2), channel_id=1, replica_groups=mesh['row'=16,'col'=32] {'col'}, use_global_device_ids=true, to_apply=%region_1.0 | all-reduce | flops 4096 | bytes 32768 | tf_op jit(solution)/shard_map/psum | solution.py:38
  177.9 0.9 concatenate.6
  178.9 0.0 copy-start.2
  178.9 1.2 convolution_bitcast_fusion.4
  180.1 73.3 %psum.37 = f32[32,64]{1,0:T(8,128)S(1)} all-reduce(f32[32,64]{1,0:T(8,128)S(1)} %convolution_bitcast_fusion.4), channel_id=1, replica_groups=mesh['row'=16,'col'=32] {'row'}, use_global_device_ids=true, to_apply=%region_2.0 | all-reduce | flops 2048 | bytes 16384 | tf_op jit(solution)/shard_map/psum | solution.py:33
  253.4 0.8 convolution_bitcast_fusion.1
  254.3 110.3 %psum.38 = f32[32,1,128]{2,0,1:T(8,128)S(1)} all-reduce(f32[32,1,128]{2,0,1:T(8,128)S(1)} %convolution_bitcast_fusion.1), channel_id=1, replica_groups=mesh['row'=16,'col'=32] {'col'}, use_global_device_ids=true, to_apply=%region_3.0 | all-reduce | flops 4096 | bytes 32768 | tf_op jit(solution)/shard_map/psum | solution.py:38
  364.6 0.0 copy-start.1
  364.6 0.7 copy-done.1
  365.3 0.0 all-gather.2.cloned.1.call-update
  365.3 0.6 copy.19
  366.0 1.2 dynamic_slice.7
  367.2 0.7 constant_dynamic-slice_fusion
  367.9 0.7 gather_fusion
  368.6 0.7 compare_convert_fusion
  369.3 60.1 %all-gather.2.cloned.1.call-done = bf16[32,400,128]{2,0,1:T(8,128)(2,1)} async-done(((bf16[32,25,128]{2,0,1:T(8,128)(2,1)}), bf16[32,400,128]{2,0,1:T(8,128)(2,1)}) %all-gather.2.cloned.1.call-update) | async-done | bytes 3276816 | tf_op jit(solution)/shard_map/all_gather | solution.py:54
  429.3 2.9 fusion.8
  432.2 0.0 copy-done
  432.2 0.3 convolution_bitcast_fusion
  432.5 43.7 %psum.39 = f32[32,128]{1,0:T(8,128)S(1)} all-reduce(f32[32,128]{1,0:T(8,128)S(1)} %convolution_bitcast_fusion), channel_id=1, replica_groups=mesh['row'=16,'col'=32] {'row'}, use_global_device_ids=true, to_apply=%region_4.5 | all-reduce | flops 4096 | bytes 32768 | tf_op jit(solution)/shard_map/psum | solution.py:64
  476.3 0.0 copy-done.2
  476.3 0.6 sub.23
  (6 shorter events, 0.0 us)
Async XLA Ops:
  7.2 425.1 %copy-start = (bf16[128,16,128]{2,1,0:T(8,128)(2,1)S(1)}, bf16[128,16,128]{2,1,0:T(8,128)(2,1)}, u32[]{:S(2)}) copy-start(bf16[128,16,128]{2,1,0:T(8,128)(2,1)} %param.14) | copy-start | bytes 1572868
  7.2 422.1 %all-gather.2.cloned.1.call-start = ((), (), s32[]{:S(2)}) async-start(), calls=%async_computation | async-start | bytes 3481600 | tf_op jit(solution)/shard_map/all_gather | solution.py:54
  178.9 297.4 %copy-start.2 = (f32[32,128]{1,0:T(8,128)S(1)}, f32[32,128]{1,0:T(8,128)}, u32[]{:S(2)}) copy-start(f32[32,128]{1,0:T(8,128)} %param.15) | copy-start | bytes 49156
  364.6 0.7 copy-start.1
Sparse Core Ops, SparseCore 0:
  365.4 63.8 all-gather.1
where the time goes:
time: 486 us; the launch traced here: 484 us
  blocking collectives  395 us (81%)
  waiting for transfers between devices  60.1 us (12%)
  between operations  14.1 us (3%)
  matrix products  7.46 us (2%)
  local copies, waits for them, and re-layouts  4.87 us (1%)
    psum x2, blocking collectives, local(): result = lax.psum(partial_share, 'col')  226 us
    psum x2, blocking collectives, local(): summed = lax.psum(partial_value, 'row')  125 us
    all_gather x1, waiting for transfers between devices, local(): section = lax.all_gather(solved_rows, 'row', axis=1, tiled=True)  60.1 us
    psum x1, blocking collectives, local(): child_total = lax.psum(child_part, 'row')  43.7 us
  transfers between devices with their start and end apart: 1, of which 1 were waited for; matrix products, arithmetic and copies ran while one was open for 1% of the time, Pallas kernels for 0%

commit v1 on v0

v1 whole, which is shorter than its diff:
```python
import functools

import jax
import jax.numpy as jnp
from jax import lax
from jax.experimental import pallas as pl
from jax.experimental.pallas import tpu as pltpu
from jax.sharding import PartitionSpec as P

MESH = pl.DeviceIdType.MESH
F32 = jnp.float32
BF16 = jnp.bfloat16
CORES = 2
ZS = 8
XS = 4
YS = 8
ROWS = ZS * CORES
NT = (((1,), (1,)), ((), ()))
NN = (((1,), (0,)), ((), ()))


def dot(a, b, dims):
    return lax.dot_general(a, b, dims, preferred_element_type=F32)


def kernel(
    u_hbm, inv_hbm, rhs_hbm, piv_hbm, below_hbm, uc_hbm, rc_hbm, map_hbm, cnt_hbm,
    x_out, c_out,
    u, inv, rhs, piv, xb, uc, rc, cmap, cnt,
    ucf, ct, cr, wsel, early,
    l10g, m0g, sy_send, sy_recv, x0y,
    p1a, p1r, p1s, p1z,
    x1p, p2, p3s, p3,
    p4a, p4r, p4s, p4z,
    p5s, p5,
    p7a, p7r, p7s, p7z,
    in_sem, send, recv,
):
    row = lax.axis_index("row")
    col = lax.axis_index("col")
    z = row // CORES
    core = lax.rem(row, CORES)
    xx = col // YS
    yy = lax.rem(col, YS)

    def at_row(d):
        return (lax.rem(row + d, ROWS), col)

    def at_z(d):
        return (lax.rem(z + d, ZS) * CORES + core, col)

    def at_x(d):
        return (row, lax.rem(xx + d, XS) * YS + yy)

    def at_y(d):
        return (row, xx * YS + lax.rem(yy + d, YS))

    sibling = (z * CORES + (1 - core), col)
    z_far_first = (4, 3, 5, 2, 6, 1, 7)
    y_far_first = (4, 3, 5, 2, 6, 1, 7)
    x_far_first = (2, 1, 3)

    barrier = pltpu.get_barrier_semaphore()
    for d in z_far_first:
        for other in (0, 1):
            pl.semaphore_signal(
                barrier, inc=1, device_id=(lax.rem(z + d, ZS) * CORES + other, col), device_id_type=MESH
            )
    for d in y_far_first:
        pl.semaphore_signal(barrier, inc=1, device_id=at_y(d), device_id_type=MESH)
    for d in x_far_first:
        pl.semaphore_signal(barrier, inc=1, device_id=at_x(d), device_id_type=MESH)
    pl.semaphore_signal(barrier, inc=1, device_id=sibling, device_id_type=MESH)

    def load(src, dst, index):
        copy = pltpu.make_async_copy(src, dst, in_sem.at[index])
        copy.start()
        return copy

    load_x = load(below_hbm, xb.at[pl.ds(2, 23)], 0)
    load_u1 = load(u_hbm.at[1], u.at[1], 1)
    load_rhs = load(rhs_hbm, rhs, 2)
    load_piv = load(piv_hbm, piv, 3)
    load_inv = load(inv_hbm, inv, 4)
    load_u0 = load(u_hbm.at[0], u.at[0], 5)
    load_uc = load(uc_hbm, uc, 6)
    load_rc = load(rc_hbm, rc, 7)
    load_map = load(map_hbm, cmap, 8)
    load_cnt = load(cnt_hbm, cnt, 9)

    def push(src, dst, phase, device):
        pltpu.make_async_remote_copy(
            src_ref=src, dst_ref=dst, send_sem=send.at[phase], recv_sem=recv.at[phase],
            device_id=device, device_id_type=MESH,
        ).start()

    def arrived(ref, phase):
        pltpu.make_async_remote_copy(
            src_ref=ref, dst_ref=ref, send_sem=send.at[phase], recv_sem=recv.at[phase],
            device_id=sibling, device_id_type=MESH,
        ).wait_recv()

    def sent(ref, phase):
        pltpu.make_async_remote_copy(
            src_ref=ref, dst_ref=ref, send_sem=send.at[phase], recv_sem=recv.at[phase],
            device_id=sibling, device_id_type=MESH,
        ).wait_send()

    xb[0] = jnp.zeros(xb.shape[1:], BF16)
    xb[1] = jnp.zeros(xb.shape[1:], BF16)

    def below_sum(panel):
        total = dot(xb[2], u[panel, 2], NT)
        for q in range(3, 25, 2):
            total += dot(
                jnp.concatenate([xb[q], xb[q + 1]], axis=1),
                jnp.concatenate([u[panel, q], u[panel, q + 1]], axis=1),
                NT,
            )
        return total

    load_x.wait()
    load_u1.wait()
    s1 = below_sum(1)
    p1a[...] = jnp.concatenate([s1[:16], s1[16:]], axis=1)
    pl.semaphore_wait(barrier, 2 * len(z_far_first) + len(y_far_first) + len(x_far_first) + 1)

    push(p1a, p1r, 0, sibling)
    load_rhs.wait()
    load_piv.wait()
    load_inv.wait()
    y1 = rhs[:, 1, :] * piv[1:2, :]
    y0 = rhs[:, 0, :] * piv[0:1, :]
    arrived(p1r, 0)
    chip = p1a[...] + p1r[...]
    p1s[...] = chip
    p1z[z] = chip
    for d in z_far_first:
        push(p1s, p1z.at[z], 1, at_z(d))

    load_u0.wait()
    for d in x_far_first:
        push(u.at[0, 1], l10g.at[d], 2, at_x(d))
        push(inv.at[0], m0g.at[d], 3, at_x(d))
    l10g[0] = u[0, 1]
    m0g[0] = inv[0]
    s0 = below_sum(0)
    sy_send[...] = jnp.concatenate([s0, y0], axis=1)
    for d in x_far_first:
        start = pl.multiple_of(lax.rem(xx + d, XS) * 8, 8)
        push(sy_send.at[pl.ds(start, 8)], sy_recv.at[d], 4, at_x(d))
    sy_recv[0] = sy_send[pl.ds(pl.multiple_of(xx * 8, 8), 8), :]
    load_uc.wait()
    ucf[...] = uc[...].astype(F32).reshape(ucf.shape)
    for d in range(16):
        ct[d] = ucf[pl.ds(d, 128, stride=16), :].astype(BF16)
    cr[0] = ct[0]

    arrived(p1z.at[pl.ds(0, 7)], 1)
    s1 = p1z[0]
    for k in range(1, ZS):
        s1 += p1z[k]
    s1 = jnp.concatenate([s1[:, :64], s1[:, 64:]], axis=0)
    t1 = (y1 - s1).astype(BF16)
    x1p[...] = dot(t1, inv[1], NN)
    for d in x_far_first:
        start = pl.multiple_of(lax.rem(xx + d, XS) * 8, 8)
        push(x1p.at[pl.ds(start, 8)], p2.at[xx], 5, at_x(d))
    p2[xx] = x1p[pl.ds(pl.multiple_of(xx * 8, 8), 8), :]
    for d in range(1, 16):
        push(ct.at[d], cr.at[d], 6, at_row(d))
    arrived(p2.at[pl.ds(0, 3)], 5)
    part = p2[0] + p2[1] + p2[2] + p2[3]
    p3s[...] = part
    p3[yy] = part
    for d in y_far_first:
        push(p3s, p3.at[yy], 7, at_y(d))

    arrived(sy_recv.at[pl.ds(1, 3)], 4)
    arrived(l10g.at[pl.ds(1, 3)], 2)
    below0 = jnp.concatenate([sy_recv[j][:, :64] for j in range(4)], axis=1)
    x0y[...] = jnp.concatenate([sy_recv[j][:, 64:] for j in range(4)], axis=1)
    l10 = l10g[...].reshape(256, 128)

    arrived(p3.at[pl.ds(0, 7)], 7)
    x1 = p3[0]
    for k in range(1, YS):
        x1 += p3[k]
    mine = pl.ds(pl.multiple_of(xx * 8, 8), 8)
    x_out[1, mine, :] = x1
    s0 = below0 + dot(x1.astype(BF16), l10, NT)
    p4a[pl.ds(0, 8), :] = s0[:, :128]
    p4a[pl.ds(8, 8), :] = s0[:, 128:]
    push(p4a, p4r, 8, sibling)
    for d in x_far_first:
        push(x_out.at[1, mine], x_out.at[1, mine], 9, at_x(d))
    arrived(m0g.at[pl.ds(1, 3)], 3)
    m0 = m0g[...].reshape(256, 128)
    arrived(p4r, 8)
    chip = p4a[...] + p4r[...]
    p4s[...] = chip
    p4z[z] = chip
    for d in z_far_first:
        push(p4s, p4z.at[z], 10, at_z(d))

    load_map.wait()
    load_cnt.wait()
    load_rc.wait()
    child = col // (XS * YS // 2)
    arrived(x_out.at[1, pl.ds(0, 24)], 9)

    arrived(p4z.at[pl.ds(0, 7)], 10)
    s0 = p4z[0]
    for k in range(1, ZS):
        s0 += p4z[k]
    t0 = (x0y[...] - jnp.concatenate([s0[:8], s0[8:]], axis=1)).astype(BF16)
    part = dot(t0, m0, NN)
    p5s[...] = part
    p5[yy] = part
    for d in y_far_first:
        push(p5s, p5.at[yy], 11, at_y(d))

    arrived(cr.at[pl.ds(1, 15)], 6)
    total = jnp.zeros((32, 128), F32)
    w0 = jnp.zeros((128, 128), F32)
    w1 = jnp.zeros((128, 128), F32)
    for d in range(16):
        slot = d * 16 + lax.rem(row - d + 16, 16)
        block = cmap[child, slot] // ROWS
        live = slot < cnt[child]
        weight = cr[d]
        term = dot(xb[block], weight, NT)
        total += jnp.where(live, term, 0.0)
        weight = weight.astype(F32)
        w0 += jnp.where(jnp.logical_and(live, block == 0), weight, 0.0)
        w1 += jnp.where(jnp.logical_and(live, block == 1), weight, 0.0)
    total += dot(x_out[1].astype(BF16), w1.astype(BF16), NT)
    w0 = w0.astype(BF16)

    arrived(p5.at[pl.ds(0, 7)], 11)
    x0 = p5[0]
    for k in range(1, YS):
        x0 += p5[k]
    x_out[0, mine, :] = x0
    for d in x_far_first:
        push(x_out.at[0, mine], x_out.at[0, mine], 12, at_x(d))
    arrived(x_out.at[0, pl.ds(0, 24)], 12)
    total += dot(x_out[0].astype(BF16), w0, NT)
    p7a[...] = total
    push(p7a, p7r, 13, sibling)
    arrived(p7r, 13)
    chip = p7a[...] + p7r[...]
    p7s[...] = chip
    p7z[z] = chip
    for d in z_far_first:
        push(p7s, p7z.at[z], 14, at_z(d))

    sent(p1a, 0)
    sent(p1z.at[pl.ds(0, 7)], 1)
    sent(l10g.at[pl.ds(1, 3)], 2)
    sent(m0g.at[pl.ds(1, 3)], 3)
    sent(sy_recv.at[pl.ds(1, 3)], 4)
    sent(p2.at[pl.ds(0, 3)], 5)
    sent(cr.at[pl.ds(1, 15)], 6)
    sent(p3.at[pl.ds(0, 7)], 7)
    sent(p4a, 8)
    sent(x_out.at[1, pl.ds(0, 24)], 9)
    sent(p4z.at[pl.ds(0, 7)], 10)
    sent(p5.at[pl.ds(0, 7)], 11)
    sent(x_out.at[0, pl.ds(0, 24)], 12)
    sent(p7a, 13)

    arrived(p7z.at[pl.ds(0, 7)], 14)
    total = p7z[0]
    for k in range(1, ZS):
        total += p7z[k]
    c_out[...] = rc[...] - total
    sent(p7z.at[pl.ds(0, 7)], 14)


def local(
    u_front,
    inverse_blocks,
    rhs_window,
    pivot_inverse,
    below_solution,
    u_child,
    rhs_child,
    child_map,
    child_counts,
):
    u = jnp.transpose(u_front, (0, 2, 1, 3))
    inv = jnp.transpose(inverse_blocks, (0, 2, 1, 3)).reshape(2, 64, 128)
    below = jnp.transpose(below_solution, (1, 0, 2))
    vm = pltpu.VMEM
    x, c = pl.pallas_call(
        kernel,
        out_shape=(
            jax.ShapeDtypeStruct((2, 32, 128), F32),
            jax.ShapeDtypeStruct((32, 128), F32),
        ),
        in_specs=[pl.BlockSpec(memory_space=pl.ANY)] * 9,
        out_specs=(pl.BlockSpec(memory_space=vm), pl.BlockSpec(memory_space=vm)),
        scratch_shapes=[
            vm((2, 25, 64, 128), BF16),
            vm((2, 64, 128), BF16),
            vm((32, 2, 64), F32),
            vm((2, 64), F32),
            vm((25, 32, 128), BF16),
            vm((128, 16, 128), BF16),
            vm((32, 128), F32),
            pltpu.SMEM((2, 256), jnp.int32),
            pltpu.SMEM((2,), jnp.int32),
            vm((2048, 128), F32),
            vm((16, 128, 128), BF16),
            vm((16, 128, 128), BF16),
            vm((2, 128, 128), BF16),
            vm((32, 128), F32),
            vm((4, 64, 128), BF16),
            vm((4, 64, 128), BF16),
            vm((32, 128), F32),
            vm((4, 8, 128), F32),
            vm((8, 256), F32),
            vm((16, 128), F32),
            vm((16, 128), F32),
            vm((16, 128), F32),
            vm((8, 16, 128), F32),
            vm((32, 128), F32),
            vm((4, 8, 128), F32),
            vm((8, 128), F32),
            vm((8, 8, 128), F32),
            vm((16, 128), F32),
            vm((16, 128), F32),
            vm((16, 128), F32),
            vm((8, 16, 128), F32),
            vm((8, 128), F32),
            vm((8, 8, 128), F32),
            vm((32, 128), F32),
            vm((32, 128), F32),
            vm((32, 128), F32),
            vm((8, 32, 128), F32),
            pltpu.SemaphoreType.DMA((10,)),
            pltpu.SemaphoreType.DMA((15,)),
            pltpu.SemaphoreType.DMA((15,)),
        ],
        compiler_params=pltpu.CompilerParams(
            collective_id=0, has_side_effects=True, vmem_limit_bytes=60 << 20
        ),
        name="solve",
    )(u, inv, rhs_window, pivot_inverse, below, u_child, rhs_child, child_map, child_counts)
    return jnp.transpose(x, (1, 0, 2)), c


def solution(mesh):
    return jax.shard_map(
        local,
        mesh=mesh,
        in_specs=(
            P(None, "col", None, "row"),
            P(None, "col", None, "row"),
            P(None, None, "col"),
            P(None, "col"),
            P(None, None, "row"),
            P("col", None, "row"),
            P(None, "col"),
            P(),
            P(),
        ),
        out_specs=(P(None, None, "row"), P(None, "col")),
        check_vma=False,
    )
```

time: 486 us -> 55.1 us (0.11)
  blocking collectives: 395 us -> 0 us
  waiting for transfers between devices: 60.1 us -> 0 us
  Pallas kernels: 0 us -> 52.2 us
  between operations: 14.1 us -> 0.65 us
  matrix products: 7.46 us -> 0 us
    psum x5 -> x0, blocking collectives: 395 us -> none  [the longest x2 226 us: local(): result = lax.psum(partial_share, 'col')]
    all_gather x1 -> x0, waiting for transfers between devices: 60.1 us -> none  [local(): section = lax.all_gather(solved_rows, 'row', axis=1, tiled=True)]
    pallas_call x0 -> x1, Pallas kernels: none -> 52.2 us  [local(): pl.pallas_call(kernel, out_shape=(jax.ShapeDtypeStruct((2, 32, 128), F32)...]
    dot_general x6 -> x0, matrix products: 7.46 us -> none  [the longest x1 2.89 us: local(): jnp.einsum('sq,nqb->nsb', selector, section, preferred_element_type=jnp.f...]
  transfers between devices with their start and end apart: 1 -> 0, of which waited for: 1 -> 0; matrix products, arithmetic and copies ran while one was open for 1% -> 0% of each run, Pallas kernels for 0% -> 0%
where the time goes in v1:
time: 55.1 us; the launch traced here: 54.9 us
  Pallas kernels  52.2 us (95%)
  local copies, waits for them, and re-layouts  2.01 us (4%)
  between operations  0.65 us (1%)
    pallas_call x1, Pallas kernels, local(): pl.pallas_call(kernel, out_shape=(jax.ShapeDtypeStruct((2, 32, 128), F32)...  52.2 us
    unnamed x4, local copies, waits for them, and re-layouts  2.01 us

profile of v1, /device:TPU:1, one launch (start us, length us, event | category | flops | bytes accessed | tf_op | source)
XLA Modules:
  0.0 54.9 jit_solution(1639361371066561792)
XLA Ops:
  0.6 52.2 %solve.1 = (f32[2,32,128]{2,1,0:T(8,128)}, f32[32,128]{1,0:T(8,128)}) custom-call(bf16[2,25,64,128]{3,2,1,0:T(8,128)(2,1)} %bitcast.4, bf16[2,64,128]{2,1,0:T(8,128)(2,1)} %bitcast.7, f32[32,2,64]{2,1,0:T(2,128)} %rhs_hbm.1, f32[2,64]{1,0:T(2,128)} %piv_hbm.1, bf16[23,32,128]{2,1,0:T(8,128)(2,1)} %bitcast.5, bf16[128,16,128]{2,1,0:T(8,128)(2,1)} %uc_hbm.1, ...), custom_call_target="tpu_custom_call" | custom-call | tf_op jit(solution)/shard_map/solve/pallas_call | solution.py:296
  52.9 0.0 copy-start
  52.9 1.4 %copy.11 = f32[32,2,128]{2,1,0:T(2,128)} copy(f32[32,2,128]{2,0,1:T(8,128)} %bitcast.6) | data formatting | bytes 65536
  54.3 0.0 copy-done
  54.3 0.6 %copy.13 = f32[32,128]{1,0:T(8,128)} copy(f32[32,128]{1,0:T(8,128)S(1)} %copy-done) | data formatting | bytes 32768
Async XLA Ops:
  52.9 1.4 %copy-start = (f32[32,128]{1,0:T(8,128)S(1)}, f32[32,128]{1,0:T(8,128)}, u32[]{:S(2)}) copy-start(f32[32,128]{1,0:T(8,128)} %get-tuple-element.11) | copy-start | bytes 49156

commit v2 on v1

v2 whole, which is shorter than its diff:
```python
import functools

import jax
import jax.numpy as jnp
from jax import lax
from jax.experimental import pallas as pl
from jax.experimental.pallas import tpu as pltpu
from jax.sharding import PartitionSpec as P

MESH = pl.DeviceIdType.MESH
F32 = jnp.float32
BF16 = jnp.bfloat16
CORES = 2
ZS = 8
XS = 4
YS = 8
ROWS = ZS * CORES
NT = (((1,), (1,)), ((), ()))
NN = (((1,), (0,)), ((), ()))


def dot(a, b, dims):
    return lax.dot_general(a, b, dims, preferred_element_type=F32)


def kernel(
    u_hbm, inv_hbm, rhs_hbm, piv_hbm, below_hbm, uc_hbm, rc_hbm, map_hbm, cnt_hbm,
    x_out, c_out,
    u, inv, rhs, piv, xb, uc, rc, cmap, cnt,
    ucf, ct, cr, xfull,
    m1g, l10g, m0g, w0s, w0g, ys, yg,
    p1s, p1r,
    p3s, p3, p4s, p4, p5s, p5,
    p6a, p6r, p6s, p6z, p7s, p7,
    in_sem, send, recv,
):
    row = lax.axis_index("row")
    col = lax.axis_index("col")
    z = row // CORES
    core = lax.rem(row, CORES)
    xx = col // YS
    yy = lax.rem(col, YS)

    def at_row(d):
        return (lax.rem(row + d, ROWS), col)

    def at_z(d):
        return (lax.rem(z + d, ZS) * CORES + core, col)

    def at_x(d):
        return (row, lax.rem(xx + d, XS) * YS + yy)

    def at_y(d):
        return (row, xx * YS + lax.rem(yy + d, YS))

    def at_row_x(dr, dx):
        return (lax.rem(row + dr, ROWS), lax.rem(xx + dx, XS) * YS + yy)

    sibling = (z * CORES + (1 - core), col)
    z_far = (4, 3, 5, 2, 6, 1, 7)
    y_far = (4, 3, 5, 2, 6, 1, 7)
    x_far = (2, 1, 3)
    row_far = (8, 9, 7, 10, 6, 11, 5, 12, 4, 13, 3, 14, 2, 15, 1)
    row_x_far = [(dr, dx) for dx in (2, 1, 3) for dr in row_far + (0,)] + [(dr, 0) for dr in row_far]

    def load(src, dst, index):
        copy = pltpu.make_async_copy(src, dst, in_sem.at[index])
        copy.start()
        return copy

    barrier = pltpu.get_barrier_semaphore()

    def greet(device):
        pl.semaphore_signal(barrier, inc=1, device_id=device, device_id_type=MESH)

    load_x = load(below_hbm, xb.at[pl.ds(2, 23)], 0)
    load_u1 = load(u_hbm.at[1], u.at[1], 1)
    for dr, dx in row_x_far:
        greet(at_row_x(dr, dx))
    for d in y_far:
        greet(at_y(d))
    load_inv = load(inv_hbm, inv, 4)
    load_rhs = load(rhs_hbm, rhs, 2)
    load_piv = load(piv_hbm, piv, 3)
    load_u0 = load(u_hbm.at[0], u.at[0], 5)
    load_uc = load(uc_hbm, uc, 6)
    load_rc = load(rc_hbm, rc, 7)
    load_map = load(map_hbm, cmap, 8)
    load_cnt = load(cnt_hbm, cnt, 9)

    def push(src, dst, phase, device):
        pltpu.make_async_remote_copy(
            src_ref=src, dst_ref=dst, send_sem=send.at[phase], recv_sem=recv.at[phase],
            device_id=device, device_id_type=MESH,
        ).start()

    def whole(ref, phase):
        return pltpu.make_async_remote_copy(
            src_ref=ref, dst_ref=ref, send_sem=send.at[phase], recv_sem=recv.at[phase],
            device_id=sibling, device_id_type=MESH,
        )

    xb[0] = jnp.zeros(xb.shape[1:], BF16)
    xb[1] = jnp.zeros(xb.shape[1:], BF16)

    def below_sum(panel):
        total = dot(xb[2], u[panel, 2], NT)
        for q in range(3, 25, 2):
            total += dot(
                jnp.concatenate([xb[q], xb[q + 1]], axis=1),
                jnp.concatenate([u[panel, q], u[panel, q + 1]], axis=1),
                NT,
            )
        return total

    load_x.wait()
    load_u1.wait()
    s1 = below_sum(1)
    load_u0.wait()
    s0 = below_sum(0)
    p1s[...] = jnp.concatenate([s1, s0], axis=1).astype(BF16).reshape(4, 8, 128)
    load_rhs.wait()
    load_piv.wait()
    load_inv.wait()
    ys[...] = jnp.concatenate([rhs[:, 1, :] * piv[1:2, :], rhs[:, 0, :] * piv[0:1, :]], axis=1)
    pl.semaphore_wait(barrier, len(row_x_far) + len(y_far))
    for dr, dx in row_x_far:
        push(p1s.at[lax.rem(xx + dx, XS)], p1r.at[dx * ROWS + row], 0, at_row_x(dr, dx))
    p1r[row] = p1s[xx]
    for d in x_far:
        push(inv.at[1], m1g.at[d], 1, at_x(d))
    for d in x_far:
        start = pl.multiple_of(lax.rem(xx + d, XS) * 8, 8)
        push(ys.at[pl.ds(start, 8)], yg.at[d], 2, at_x(d))
    mine = pl.ds(pl.multiple_of(xx * 8, 8), 8)
    m1g[0] = inv[1]
    yg[0] = ys[mine, :]

    for d in x_far:
        push(u.at[0, 1], l10g.at[d], 4, at_x(d))
    for d in x_far:
        push(inv.at[0], m0g.at[d], 5, at_x(d))
    l10g[0] = u[0, 1]
    m0g[0] = inv[0]
    load_uc.wait()
    ucf[...] = uc[...].astype(F32).reshape(ucf.shape)
    for d in range(16):
        ct[d] = ucf[pl.ds(d, 128, stride=16), :].astype(BF16)
    cr[0] = ct[0]
    for d in row_far:
        push(ct.at[d], cr.at[d], 7, at_row(d))
    whole(yg.at[pl.ds(1, 3)], 2).wait_recv()
    y1 = jnp.concatenate([yg[j][:, :64] for j in range(XS)], axis=1)
    y0 = jnp.concatenate([yg[j][:, 64:] for j in range(XS)], axis=1)
    whole(m1g.at[pl.ds(1, 3)], 1).wait_recv()

    whole(p1r.at[pl.ds(0, 63)], 0).wait_recv()
    below = []
    for j in range(XS):
        total = p1r[j * ROWS].astype(F32)
        for k in range(1, ROWS):
            total += p1r[j * ROWS + k].astype(F32)
        below.append(total)
    t1 = (y1 - jnp.concatenate([v[:, :64] for v in below], axis=1)).astype(BF16)
    part = dot(t1, m1g[...].reshape(256, 128), NN)
    p3s[...] = part
    p3[yy] = part
    for d in y_far:
        push(p3s, p3.at[yy], 6, at_y(d))
    y0 = y0 - jnp.concatenate([v[:, 64:] for v in below], axis=1)
    whole(l10g.at[pl.ds(1, 3)], 4).wait_recv()
    whole(m0g.at[pl.ds(1, 3)], 5).wait_recv()

    whole(p3.at[pl.ds(0, 7)], 6).wait_recv()
    x1 = p3[0]
    for k in range(1, YS):
        x1 += p3[k]
    xfull[1, mine, :] = x1
    s0 = dot(x1.astype(BF16), l10g[...].reshape(256, 128), NT).astype(BF16)
    p4s[pl.ds(0, 8), :] = s0[:, :128]
    p4s[pl.ds(8, 8), :] = s0[:, 128:]
    for d in row_far:
        push(p4s, p4.at[row], 8, at_row(d))
    p4[row] = p4s[...]
    for d in x_far:
        push(xfull.at[1, mine], xfull.at[1, mine], 9, at_x(d))

    load_map.wait()
    load_cnt.wait()
    load_rc.wait()
    child = col // (XS * YS // 2)
    whole(cr.at[pl.ds(1, 15)], 7).wait_recv()
    w0 = jnp.zeros((128, 128), F32)
    for d in range(16):
        slot = d * 16 + lax.rem(row - d + 16, 16)
        wanted = jnp.logical_and(slot < cnt[child], cmap[child, slot] // ROWS == 0)
        w0 += jnp.where(wanted, cr[d].astype(F32), 0.0)
    w0s[...] = w0.astype(BF16)
    w0g[0] = w0s[...]
    for d in x_far:
        push(w0s, w0g.at[d], 10, at_x(d))

    whole(p4.at[pl.ds(0, 15)], 8).wait_recv()
    s0 = p4[0].astype(F32)
    for k in range(1, ROWS):
        s0 += p4[k].astype(F32)
    t0 = (y0 - jnp.concatenate([s0[:8], s0[8:]], axis=1)).astype(BF16)
    part = dot(t0, m0g[...].reshape(256, 128), NN)
    p5s[...] = part
    p5[yy] = part
    for d in y_far:
        push(p5s, p5.at[yy], 11, at_y(d))

    whole(xfull.at[1, pl.ds(0, 24)], 9).wait_recv()
    x1 = xfull[1]
    x_out[:, 1, :] = x1
    xb[1] = x1.astype(BF16)
    total = jnp.zeros((32, 128), F32)
    for d in range(16):
        slot = d * 16 + lax.rem(row - d + 16, 16)
        term = dot(xb[cmap[child, slot] // ROWS], cr[d], NT)
        total += jnp.where(slot < cnt[child], term, 0.0)
    p6a[...] = total
    push(p6a, p6r, 12, sibling)
    whole(w0g.at[pl.ds(1, 3)], 10).wait_recv()
    whole(p6r, 12).wait_recv()
    chip = (p6a[...] + p6r[...]).astype(BF16)
    p6s[...] = chip
    p6z[z] = chip
    for d in z_far:
        push(p6s, p6z.at[z], 13, at_z(d))

    whole(p5.at[pl.ds(0, 7)], 11).wait_recv()
    x0 = p5[0]
    for k in range(1, YS):
        x0 += p5[k]
    late = dot(x0.astype(BF16), w0g[...].reshape(512, 128), NT).astype(BF16)
    for j in range(XS):
        p7s[j] = late[:, 128 * j:128 * j + 128]
    for dr, dx in row_x_far:
        push(p7s.at[(XS - dx) % XS], p7.at[xx * ROWS + row], 14, at_row_x(dr, dx))
    p7[xx * ROWS + row] = p7s[0]
    xfull[0, mine, :] = x0
    for d in x_far:
        push(xfull.at[0, mine], xfull.at[0, mine], 15, at_x(d))

    whole(p1r.at[pl.ds(0, 63)], 0).wait_send()
    whole(m1g.at[pl.ds(1, 3)], 1).wait_send()
    whole(yg.at[pl.ds(1, 3)], 2).wait_send()
    whole(l10g.at[pl.ds(1, 3)], 4).wait_send()
    whole(m0g.at[pl.ds(1, 3)], 5).wait_send()
    whole(p3.at[pl.ds(0, 7)], 6).wait_send()
    whole(cr.at[pl.ds(1, 15)], 7).wait_send()
    whole(p4.at[pl.ds(0, 15)], 8).wait_send()
    whole(xfull.at[1, pl.ds(0, 24)], 9).wait_send()
    whole(w0g.at[pl.ds(1, 3)], 10).wait_send()
    whole(p5.at[pl.ds(0, 7)], 11).wait_send()
    whole(p6r, 12).wait_send()
    whole(p6z.at[pl.ds(0, 7)], 13).wait_send()

    whole(p6z.at[pl.ds(0, 7)], 13).wait_recv()
    total = p6z[0].astype(F32)
    for k in range(1, ZS):
        total += p6z[k].astype(F32)
    total = rc[...] - total
    whole(xfull.at[0, pl.ds(0, 24)], 15).wait()
    x_out[:, 0, :] = xfull[0]

    whole(p7.at[pl.ds(0, 63)], 14).wait()
    for j in range(XS):
        late = p7[j * ROWS].astype(F32)
        for k in range(1, ROWS):
            late += p7[j * ROWS + k].astype(F32)
        c_out[pl.ds(8 * j, 8), :] = total[8 * j:8 * j + 8] - late


def local(
    u_front,
    inverse_blocks,
    rhs_window,
    pivot_inverse,
    below_solution,
    u_child,
    rhs_child,
    child_map,
    child_counts,
):
    u = jnp.transpose(u_front, (0, 2, 1, 3))
    inv = jnp.transpose(inverse_blocks, (0, 2, 1, 3)).reshape(2, 64, 128)
    below = jnp.transpose(below_solution, (1, 0, 2))
    vm = pltpu.VMEM
    return pl.pallas_call(
        kernel,
        out_shape=(
            jax.ShapeDtypeStruct((32, 2, 128), F32),
            jax.ShapeDtypeStruct((32, 128), F32),
        ),
        in_specs=[pl.BlockSpec(memory_space=pl.ANY)] * 9,
        out_specs=(pl.BlockSpec(memory_space=vm), pl.BlockSpec(memory_space=vm)),
        scratch_shapes=[
            vm((2, 25, 64, 128), BF16),
            vm((2, 64, 128), BF16),
            vm((32, 2, 64), F32),
            vm((2, 64), F32),
            vm((25, 32, 128), BF16),
            vm((128, 16, 128), BF16),
            vm((32, 128), F32),
            pltpu.SMEM((2, 256), jnp.int32),
            pltpu.SMEM((2,), jnp.int32),
            vm((2048, 128), F32),
            vm((16, 128, 128), BF16),
            vm((16, 128, 128), BF16),
            vm((2, 32, 128), F32),
            vm((4, 64, 128), BF16),
            vm((4, 64, 128), BF16),
            vm((4, 64, 128), BF16),
            vm((128, 128), BF16),
            vm((4, 128, 128), BF16),
            vm((32, 128), F32),
            vm((4, 8, 128), F32),
            vm((4, 8, 128), BF16),
            vm((64, 8, 128), BF16),
            vm((8, 128), F32),
            vm((8, 8, 128), F32),
            vm((16, 128), BF16),
            vm((16, 16, 128), BF16),
            vm((8, 128), F32),
            vm((8, 8, 128), F32),
            vm((32, 128), F32),
            vm((32, 128), F32),
            vm((32, 128), BF16),
            vm((8, 32, 128), BF16),
            vm((4, 8, 128), BF16),
            vm((64, 8, 128), BF16),
            pltpu.SemaphoreType.DMA((10,)),
            pltpu.SemaphoreType.DMA((16,)),
            pltpu.SemaphoreType.DMA((16,)),
        ],
        compiler_params=pltpu.CompilerParams(
            collective_id=0, has_side_effects=True, vmem_limit_bytes=60 << 20
        ),
        name="solve",
    )(u, inv, rhs_window, pivot_inverse, below, u_child, rhs_child, child_map, child_counts)


def solution(mesh):
    return jax.shard_map(
        local,
        mesh=mesh,
        in_specs=(
            P(None, "col", None, "row"),
            P(None, "col", None, "row"),
            P(None, None, "col"),
            P(None, "col"),
            P(None, None, "row"),
            P("col", None, "row"),
            P(None, "col"),
            P(),
            P(),
        ),
        out_specs=(P(None, None, "row"), P(None, "col")),
        check_vma=False,
    )
```

time: 55.1 us -> 50.4 us (0.915)
  Pallas kernels: 52.2 us -> 47.6 us
    pallas_call x1, Pallas kernels: 52.2 us -> 47.6 us  [local(): pl.pallas_call(kernel, out_shape=(jax.ShapeDtypeStruct((32, 2, 128), F32)...]
where the time goes in v2:
time: 50.4 us; the launch traced here: 50.2 us
  Pallas kernels  47.6 us (94%)
  local copies, waits for them, and re-layouts  1.99 us (4%)
  between operations  0.65 us (1%)
    pallas_call x1, Pallas kernels, local(): pl.pallas_call(kernel, out_shape=(jax.ShapeDtypeStruct((32, 2, 128), F32)...  47.6 us
    unnamed x4, local copies, waits for them, and re-layouts  1.99 us

profile of v2, /device:TPU:1, one launch (start us, length us, event | category | flops | bytes accessed | tf_op | source)
XLA Modules:
  0.0 50.2 jit_solution(13260653528505863450)
XLA Ops:
  0.6 47.6 %solve.1 = (f32[32,2,128]{2,1,0:T(2,128)}, f32[32,128]{1,0:T(8,128)}) custom-call(bf16[2,25,64,128]{3,2,1,0:T(8,128)(2,1)} %bitcast.3, bf16[2,64,128]{2,1,0:T(8,128)(2,1)} %bitcast.5, f32[32,2,64]{2,1,0:T(2,128)} %rhs_hbm.1, f32[2,64]{1,0:T(2,128)} %piv_hbm.1, bf16[23,32,128]{2,1,0:T(8,128)(2,1)} %bitcast.4, bf16[128,16,128]{2,1,0:T(8,128)(2,1)} %uc_hbm.1, ...), custom_call_target="tpu_custom_call" | custom-call | tf_op jit(solution)/shard_map/solve/pallas_call | solution.py:292
  48.2 0.0 copy-start
  48.2 1.4 %copy.13 = f32[32,2,128]{2,1,0:T(2,128)} copy(f32[32,2,128]{2,1,0:T(2,128)} %get-tuple-element.4) | data formatting | bytes 65536
  49.6 0.0 copy-done
  49.6 0.6 %copy.14 = f32[32,128]{1,0:T(8,128)} copy(f32[32,128]{1,0:T(8,128)S(1)} %copy-done) | data formatting | bytes 32768
Async XLA Ops:
  48.2 1.4 %copy-start = (f32[32,128]{1,0:T(8,128)S(1)}, f32[32,128]{1,0:T(8,128)}, u32[]{:S(2)}) copy-start(f32[32,128]{1,0:T(8,128)} %get-tuple-element.5) | copy-start | bytes 49156

commit v3 on v2

--- a/solution.py
+++ b/solution.py
@@ -28,7 +28,7 @@
     x_out, c_out,
     u, inv, rhs, piv, xb, uc, rc, cmap, cnt,
     ucf, ct, cr, xfull,
-    m1g, l10g, m0g, w0s, w0g, ys, yg,
+    m1g, l10g, m0g, w0s, w0g, ys, yg, ss, sg,
     p1s, p1r,
     p3s, p3, p4s, p4, p5s, p5,
     p6a, p6r, p6s, p6z, p7s, p7,
@@ -116,9 +116,8 @@
     load_x.wait()
     load_u1.wait()
     s1 = below_sum(1)
-    load_u0.wait()
-    s0 = below_sum(0)
-    p1s[...] = jnp.concatenate([s1, s0], axis=1).astype(BF16).reshape(4, 8, 128)
+    for k in range(XS):
+        p1s[k] = jnp.concatenate([s1[8 * k:8 * k + 4], s1[8 * k + 4:8 * k + 8]], axis=1).astype(BF16)
     load_rhs.wait()
     load_piv.wait()
     load_inv.wait()
@@ -136,38 +135,55 @@
     m1g[0] = inv[1]
     yg[0] = ys[mine, :]
 
-    for d in x_far:
-        push(u.at[0, 1], l10g.at[d], 4, at_x(d))
-    for d in x_far:
-        push(inv.at[0], m0g.at[d], 5, at_x(d))
-    l10g[0] = u[0, 1]
-    m0g[0] = inv[0]
     load_uc.wait()
     ucf[...] = uc[...].astype(F32).reshape(ucf.shape)
     for d in range(16):
         ct[d] = ucf[pl.ds(d, 128, stride=16), :].astype(BF16)
     cr[0] = ct[0]
-    for d in row_far:
+    for d in (5, 11, 6, 10, 7, 9, 8):
         push(ct.at[d], cr.at[d], 7, at_row(d))
+    load_u0.wait()
+    for d in x_far:
+        push(u.at[0, 1], l10g.at[d], 4, at_x(d))
+    for d in x_far:
+        push(inv.at[0], m0g.at[d], 5, at_x(d))
+    l10g[0] = u[0, 1]
+    m0g[0] = inv[0]
+    s0 = below_sum(0)
+    ss[...] = jnp.concatenate([s0, s0], axis=1)
+    for d in x_far:
+        start = pl.multiple_of(lax.rem(xx + d, XS) * 8, 8)
+        push(ss.at[pl.ds(start, 8)], sg.at[d], 3, at_x(d))
+    sg[0] = ss[mine, :]
     whole(yg.at[pl.ds(1, 3)], 2).wait_recv()
     y1 = jnp.concatenate([yg[j][:, :64] for j in range(XS)], axis=1)
     y0 = jnp.concatenate([yg[j][:, 64:] for j in range(XS)], axis=1)
     whole(m1g.at[pl.ds(1, 3)], 1).wait_recv()
 
     whole(p1r.at[pl.ds(0, 63)], 0).wait_recv()
-    below = []
+    sums = []
     for j in range(XS):
         total = p1r[j * ROWS].astype(F32)
         for k in range(1, ROWS):
             total += p1r[j * ROWS + k].astype(F32)
-        below.append(total)
-    t1 = (y1 - jnp.concatenate([v[:, :64] for v in below], axis=1)).astype(BF16)
+        sums.append(total)
+    s1 = jnp.concatenate(
+        [
+            jnp.concatenate([v[:, :64] for v in sums], axis=1),
+            jnp.concatenate([v[:, 64:] for v in sums], axis=1),
+        ],
+        axis=0,
+    )
+    t1 = (y1 - s1).astype(BF16)
     part = dot(t1, m1g[...].reshape(256, 128), NN)
     p3s[...] = part
     p3[yy] = part
     for d in y_far:
         push(p3s, p3.at[yy], 6, at_y(d))
-    y0 = y0 - jnp.concatenate([v[:, 64:] for v in below], axis=1)
+    for d in (1, 15, 2, 14, 3, 13, 4, 12):
+        push(ct.at[d], cr.at[d], 7, at_row(d))
+    whole(sg.at[pl.ds(1, 3)], 3).wait_recv()
+    below0 = jnp.concatenate([sg[j][:, :64] for j in range(XS)], axis=1)
     whole(l10g.at[pl.ds(1, 3)], 4).wait_recv()
     whole(m0g.at[pl.ds(1, 3)], 5).wait_recv()
 
@@ -176,7 +192,7 @@
     for k in range(1, YS):
         x1 += p3[k]
     xfull[1, mine, :] = x1
-    s0 = dot(x1.astype(BF16), l10g[...].reshape(256, 128), NT).astype(BF16)
+    s0 = (below0 + dot(x1.astype(BF16), l10g[...].reshape(256, 128), NT)).astype(BF16)
     p4s[pl.ds(0, 8), :] = s0[:, :128]
     p4s[pl.ds(8, 8), :] = s0[:, 128:]
     for d in row_far:
@@ -247,6 +263,7 @@
     whole(p1r.at[pl.ds(0, 63)], 0).wait_send()
     whole(m1g.at[pl.ds(1, 3)], 1).wait_send()
     whole(yg.at[pl.ds(1, 3)], 2).wait_send()
+    whole(sg.at[pl.ds(1, 3)], 3).wait_send()
     whole(l10g.at[pl.ds(1, 3)], 4).wait_send()
     whole(m0g.at[pl.ds(1, 3)], 5).wait_send()
     whole(p3.at[pl.ds(0, 7)], 6).wait_send()
@@ -318,8 +335,10 @@
             vm((4, 128, 128), BF16),
             vm((32, 128), F32),
             vm((4, 8, 128), F32),
-            vm((4, 8, 128), BF16),
-            vm((64, 8, 128), BF16),
+            vm((32, 128), F32),
+            vm((4, 8, 128), F32),
+            vm((4, 4, 128), BF16),
+            vm((64, 4, 128), BF16),
             vm((8, 128), F32),
             vm((8, 8, 128), F32),
             vm((16, 128), BF16),

time: 50.4 us -> 48.4 us (0.960)
  Pallas kernels: 47.6 us -> 45.6 us
    pallas_call x1, Pallas kernels: 47.6 us -> 45.6 us  [local(): pl.pallas_call(kernel, out_shape=(jax.ShapeDtypeStruct((32, 2, 128), F32)...]
where the time goes in v3:
time: 48.4 us; the launch traced here: 48.2 us
  Pallas kernels  45.6 us (94%)
  local copies, waits for them, and re-layouts  1.99 us (4%)
  between operations  0.65 us (1%)
    pallas_call x1, Pallas kernels, local(): pl.pallas_call(kernel, out_shape=(jax.ShapeDtypeStruct((32, 2, 128), F32)...  45.6 us
    unnamed x4, local copies, waits for them, and re-layouts  1.99 us

profile of v3, /device:TPU:1, one launch (start us, length us, event | category | flops | bytes accessed | tf_op | source)
XLA Modules:
  0.0 48.2 jit_solution(11476627014266898892)
XLA Ops:
  0.6 45.6 %solve.1 = (f32[32,2,128]{2,1,0:T(2,128)}, f32[32,128]{1,0:T(8,128)}) custom-call(bf16[2,25,64,128]{3,2,1,0:T(8,128)(2,1)} %bitcast.3, bf16[2,64,128]{2,1,0:T(8,128)(2,1)} %bitcast.5, f32[32,2,64]{2,1,0:T(2,128)} %rhs_hbm.1, f32[2,64]{1,0:T(2,128)} %piv_hbm.1, bf16[23,32,128]{2,1,0:T(8,128)(2,1)} %bitcast.4, bf16[128,16,128]{2,1,0:T(8,128)(2,1)} %uc_hbm.1, ...), custom_call_target="tpu_custom_call" | custom-call | tf_op jit(solution)/shard_map/solve/pallas_call | solution.py:309
  46.2 0.0 copy-start
  46.2 1.4 %copy.13 = f32[32,2,128]{2,1,0:T(2,128)} copy(f32[32,2,128]{2,1,0:T(2,128)} %get-tuple-element.4) | data formatting | bytes 65536
  47.6 0.0 copy-done
  47.6 0.6 %copy.14 = f32[32,128]{1,0:T(8,128)} copy(f32[32,128]{1,0:T(8,128)S(1)} %copy-done) | data formatting | bytes 32768
Async XLA Ops:
  46.2 1.4 %copy-start = (f32[32,128]{1,0:T(8,128)S(1)}, f32[32,128]{1,0:T(8,128)}, u32[]{:S(2)}) copy-start(f32[32,128]{1,0:T(8,128)} %get-tuple-element.5) | copy-start | bytes 49156

commit v4 on v3

--- a/solution.py
+++ b/solution.py
@@ -28,11 +28,11 @@
     x_out, c_out,
     u, inv, rhs, piv, xb, uc, rc, cmap, cnt,
     ucf, ct, cr, xfull,
-    m1g, l10g, m0g, w0s, w0g, ys, yg, ss, sg,
+    l10g, m0g, w0s, w0g, ss, sg,
     p1s, p1r,
     p3s, p3, p4s, p4, p5s, p5,
     p6a, p6r, p6s, p6z, p7s, p7,
-    in_sem, send, recv,
+    in_sem, send, recv, ready,
 ):
     row = lax.axis_index("row")
     col = lax.axis_index("col")
@@ -56,11 +56,15 @@
     def at_row_x(dr, dx):
         return (lax.rem(row + dr, ROWS), lax.rem(xx + dx, XS) * YS + yy)
 
+    def at_col(dx, dy):
+        return (row, lax.rem(xx + dx, XS) * YS + lax.rem(yy + dy, YS))
+
     sibling = (z * CORES + (1 - core), col)
     z_far = (4, 3, 5, 2, 6, 1, 7)
     y_far = (4, 3, 5, 2, 6, 1, 7)
     x_far = (2, 1, 3)
     row_far = (8, 9, 7, 10, 6, 11, 5, 12, 4, 13, 3, 14, 2, 15, 1)
+    col_far = [(dx, dy) for dx in (2, 1, 3) for dy in (4, 3, 5, 2, 6, 1, 7, 0)] + [(0, dy) for dy in (4, 3, 5, 2, 6, 1, 7)]
     row_x_far = [(dr, dx) for dx in (2, 1, 3) for dr in row_far + (0,)] + [(dr, 0) for dr in row_far]
 
     def load(src, dst, index):
@@ -75,13 +79,15 @@
 
     load_x = load(below_hbm, xb.at[pl.ds(2, 23)], 0)
     load_u1 = load(u_hbm.at[1], u.at[1], 1)
-    for dr, dx in row_x_far:
-        greet(at_row_x(dr, dx))
+    for d in row_far:
+        greet(at_row(d))
     for d in y_far:
         greet(at_y(d))
-    load_inv = load(inv_hbm, inv, 4)
+    for d in x_far:
+        greet(at_x(d))
     load_rhs = load(rhs_hbm, rhs, 2)
     load_piv = load(piv_hbm, piv, 3)
+    load_inv = load(inv_hbm, inv, 4)
     load_u0 = load(u_hbm.at[0], u.at[0], 5)
     load_uc = load(uc_hbm, uc, 6)
     load_rc = load(rc_hbm, rc, 7)
@@ -116,31 +122,26 @@
     load_x.wait()
     load_u1.wait()
     s1 = below_sum(1)
-    for k in range(XS):
-        p1s[k] = jnp.concatenate([s1[8 * k:8 * k + 4], s1[8 * k + 4:8 * k + 8]], axis=1).astype(BF16)
+    p1s[...] = jnp.concatenate([s1[:16], s1[16:]], axis=1).astype(BF16)
+    pl.semaphore_wait(barrier, len(row_far) + len(y_far) + len(x_far))
+    for d in row_far:
+        push(p1s, p1r.at[row], 0, at_row(d))
+    p1r[row] = p1s[...]
+    for d in x_far:
+        pl.semaphore_signal(ready, inc=1, device_id=at_x(d), device_id_type=MESH)
     load_rhs.wait()
     load_piv.wait()
     load_inv.wait()
-    ys[...] = jnp.concatenate([rhs[:, 1, :] * piv[1:2, :], rhs[:, 0, :] * piv[0:1, :]], axis=1)
-    pl.semaphore_wait(barrier, len(row_x_far) + len(y_far))
-    for dr, dx in row_x_far:
-        push(p1s.at[lax.rem(xx + dx, XS)], p1r.at[dx * ROWS + row], 0, at_row_x(dr, dx))
-    p1r[row] = p1s[xx]
-    for d in x_far:
-        push(inv.at[1], m1g.at[d], 1, at_x(d))
-    for d in x_far:
-        start = pl.multiple_of(lax.rem(xx + d, XS) * 8, 8)
-        push(ys.at[pl.ds(start, 8)], yg.at[d], 2, at_x(d))
+    y1 = rhs[:, 1, :] * piv[1:2, :]
+    y0 = rhs[:, 0, :] * piv[0:1, :]
     mine = pl.ds(pl.multiple_of(xx * 8, 8), 8)
-    m1g[0] = inv[1]
-    yg[0] = ys[mine, :]
 
     load_uc.wait()
     ucf[...] = uc[...].astype(F32).reshape(ucf.shape)
     for d in range(16):
         ct[d] = ucf[pl.ds(d, 128, stride=16), :].astype(BF16)
     cr[0] = ct[0]
-    for d in (5, 11, 6, 10, 7, 9, 8):
+    for d in (13, 4, 12, 5, 11, 6, 10, 7, 9, 8):
         push(ct.at[d], cr.at[d], 7, at_row(d))
     load_u0.wait()
     for d in x_far:
@@ -150,47 +151,35 @@
     l10g[0] = u[0, 1]
     m0g[0] = inv[0]
     s0 = below_sum(0)
-    ss[...] = jnp.concatenate([s0, s0], axis=1)
+    ss[...] = jnp.concatenate([s0, y0], axis=1)
     for d in x_far:
         start = pl.multiple_of(lax.rem(xx + d, XS) * 8, 8)
         push(ss.at[pl.ds(start, 8)], sg.at[d], 3, at_x(d))
     sg[0] = ss[mine, :]
-    whole(yg.at[pl.ds(1, 3)], 2).wait_recv()
-    y1 = jnp.concatenate([yg[j][:, :64] for j in range(XS)], axis=1)
-    y0 = jnp.concatenate([yg[j][:, 64:] for j in range(XS)], axis=1)
-    whole(m1g.at[pl.ds(1, 3)], 1).wait_recv()
-
-    whole(p1r.at[pl.ds(0, 63)], 0).wait_recv()
-    sums = []
-    for j in range(XS):
-        total = p1r[j * ROWS].astype(F32)
-        for k in range(1, ROWS):
-            total += p1r[j * ROWS + k].astype(F32)
-        sums.append(total)
-    s1 = jnp.concatenate(
-        [
-            jnp.concatenate([v[:, :64] for v in sums], axis=1),
-            jnp.concatenate([v[:, 64:] for v in sums], axis=1),
-        ],
-        axis=0,
-    )
-    t1 = (y1 - s1).astype(BF16)
-    part = dot(t1, m1g[...].reshape(256, 128), NN)
-    p3s[...] = part
-    p3[yy] = part
-    for d in y_far:
-        push(p3s, p3.at[yy], 6, at_y(d))
-    for d in (1, 15, 2, 14, 3, 13, 4, 12):
+    pl.semaphore_wait(ready, len(x_far))
+
+    whole(p1r.at[pl.ds(0, 15)], 0).wait_recv()
+    s1 = p1r[0].astype(F32)
+    for k in range(1, ROWS):
+        s1 += p1r[k].astype(F32)
+    s1 = jnp.concatenate([s1[:, :64], s1[:, 64:]], axis=0)
+    part = dot((y1 - s1).astype(BF16), inv[1], NN).astype(p3s.dtype)
+    p3s[...] = part.reshape(4, 8, 128)
+    for dx, dy in col_far:
+        push(p3s.at[lax.rem(xx + dx, XS)], p3.at[col], 6, at_col(dx, dy))
+    p3[col] = p3s[xx]
+    for d in (1, 15, 2, 14, 3):
         push(ct.at[d], cr.at[d], 7, at_row(d))
     whole(sg.at[pl.ds(1, 3)], 3).wait_recv()
     below0 = jnp.concatenate([sg[j][:, :64] for j in range(XS)], axis=1)
+    y0 = jnp.concatenate([sg[j][:, 64:] for j in range(XS)], axis=1)
     whole(l10g.at[pl.ds(1, 3)], 4).wait_recv()
     whole(m0g.at[pl.ds(1, 3)], 5).wait_recv()
 
-    whole(p3.at[pl.ds(0, 7)], 6).wait_recv()
-    x1 = p3[0]
-    for k in range(1, YS):
-        x1 += p3[k]
+    whole(p3.at[pl.ds(0, 31)], 6).wait_recv()
+    x1 = p3[0].astype(F32)
+    for k in range(1, XS * YS):
+        x1 += p3[k].astype(F32)
     xfull[1, mine, :] = x1
     s0 = (below0 + dot(x1.astype(BF16), l10g[...].reshape(256, 128), NT)).astype(BF16)
     p4s[pl.ds(0, 8), :] = s0[:, :128]
@@ -260,13 +249,11 @@
     for d in x_far:
         push(xfull.at[0, mine], xfull.at[0, mine], 15, at_x(d))
 
-    whole(p1r.at[pl.ds(0, 63)], 0).wait_send()
-    whole(m1g.at[pl.ds(1, 3)], 1).wait_send()
-    whole(yg.at[pl.ds(1, 3)], 2).wait_send()
+    whole(p1r.at[pl.ds(0, 15)], 0).wait_send()
     whole(sg.at[pl.ds(1, 3)], 3).wait_send()
     whole(l10g.at[pl.ds(1, 3)], 4).wait_send()
     whole(m0g.at[pl.ds(1, 3)], 5).wait_send()
-    whole(p3.at[pl.ds(0, 7)], 6).wait_send()
+    whole(p3.at[pl.ds(0, 31)], 6).wait_send()
     whole(cr.at[pl.ds(1, 15)], 7).wait_send()
     whole(p4.at[pl.ds(0, 15)], 8).wait_send()
     whole(xfull.at[1, pl.ds(0, 24)], 9).wait_send()
@@ -330,17 +317,14 @@
             vm((2, 32, 128), F32),
             vm((4, 64, 128), BF16),
             vm((4, 64, 128), BF16),
-            vm((4, 64, 128), BF16),
             vm((128, 128), BF16),
             vm((4, 128, 128), BF16),
             vm((32, 128), F32),
             vm((4, 8, 128), F32),
-            vm((32, 128), F32),
+            vm((16, 128), BF16),
+            vm((16, 16, 128), BF16),
             vm((4, 8, 128), F32),
-            vm((4, 4, 128), BF16),
-            vm((64, 4, 128), BF16),
-            vm((8, 128), F32),
-            vm((8, 8, 128), F32),
+            vm((32, 8, 128), F32),
             vm((16, 128), BF16),
             vm((16, 16, 128), BF16),
             vm((8, 128), F32),
@@ -354,6 +338,7 @@
             pltpu.SemaphoreType.DMA((10,)),
             pltpu.SemaphoreType.DMA((16,)),
             pltpu.SemaphoreType.DMA((16,)),
+            pltpu.SemaphoreType.REGULAR,
         ],
         compiler_params=pltpu.CompilerParams(
             collective_id=0, has_side_effects=True, vmem_limit_bytes=60 << 20

time: 48.4 us -> 47.5 us (0.981)
  Pallas kernels: 45.6 us -> 44.6 us
    pallas_call x1, Pallas kernels: 45.6 us -> 44.6 us  [local(): pl.pallas_call(kernel, out_shape=(jax.ShapeDtypeStruct((32, 2, 128), F32)...]
where the time goes in v4:
time: 47.5 us; the launch traced here: 47.3 us
  Pallas kernels  44.6 us (94%)
  local copies, waits for them, and re-layouts  1.99 us (4%)
  between operations  0.65 us (1%)
    pallas_call x1, Pallas kernels, local(): pl.pallas_call(kernel, out_shape=(jax.ShapeDtypeStruct((32, 2, 128), F32)...  44.6 us
    unnamed x4, local copies, waits for them, and re-layouts  1.99 us

profile of v4, /device:TPU:1, one launch (start us, length us, event | category | flops | bytes accessed | tf_op | source)
XLA Modules:
  0.0 47.3 jit_solution(14305476500144236699)
XLA Ops:
  0.6 44.6 %solve.1 = (f32[32,2,128]{2,1,0:T(2,128)}, f32[32,128]{1,0:T(8,128)}) custom-call(bf16[2,25,64,128]{3,2,1,0:T(8,128)(2,1)} %bitcast.3, bf16[2,64,128]{2,1,0:T(8,128)(2,1)} %bitcast.5, f32[32,2,64]{2,1,0:T(2,128)} %rhs_hbm.1, f32[2,64]{1,0:T(2,128)} %piv_hbm.1, bf16[23,32,128]{2,1,0:T(8,128)(2,1)} %bitcast.4, bf16[128,16,128]{2,1,0:T(8,128)(2,1)} %uc_hbm.1, ...), custom_call_target="tpu_custom_call" | custom-call | tf_op jit(solution)/shard_map/solve/pallas_call | solution.py:296
  45.3 0.0 copy-start
  45.3 1.4 %copy.13 = f32[32,2,128]{2,1,0:T(2,128)} copy(f32[32,2,128]{2,1,0:T(2,128)} %get-tuple-element.4) | data formatting | bytes 65536
  46.7 0.0 copy-done
  46.7 0.6 %copy.14 = f32[32,128]{1,0:T(8,128)} copy(f32[32,128]{1,0:T(8,128)S(1)} %copy-done) | data formatting | bytes 32768
Async XLA Ops:
  45.3 1.4 %copy-start = (f32[32,128]{1,0:T(8,128)S(1)}, f32[32,128]{1,0:T(8,128)}, u32[]{:S(2)}) copy-start(f32[32,128]{1,0:T(8,128)} %get-tuple-element.5) | copy-start | bytes 49156

commit v5 on v4

--- a/solution.py
+++ b/solution.py
@@ -25,14 +25,14 @@
 
 def kernel(
     u_hbm, inv_hbm, rhs_hbm, piv_hbm, below_hbm, uc_hbm, rc_hbm, map_hbm, cnt_hbm,
-    x_out, c_out,
+    x_hbm, c_hbm,
     u, inv, rhs, piv, xb, uc, rc, cmap, cnt,
     ucf, ct, cr, xfull,
     l10g, m0g, w0s, w0g, ss, sg,
     p1s, p1r,
     p3s, p3, p4s, p4, p5s, p5,
-    p6a, p6r, p6s, p6z, p7s, p7,
-    in_sem, send, recv, ready,
+    p6s, p6, p7s, p7,
+    x_out, c_out, in_sem, send, recv, ready,
 ):
     row = lax.axis_index("row")
     col = lax.axis_index("col")
@@ -44,9 +44,6 @@
     def at_row(d):
         return (lax.rem(row + d, ROWS), col)
 
-    def at_z(d):
-        return (lax.rem(z + d, ZS) * CORES + core, col)
-
     def at_x(d):
         return (row, lax.rem(xx + d, XS) * YS + yy)
 
@@ -60,7 +57,6 @@
         return (row, lax.rem(xx + dx, XS) * YS + lax.rem(yy + dy, YS))
 
     sibling = (z * CORES + (1 - core), col)
-    z_far = (4, 3, 5, 2, 6, 1, 7)
     y_far = (4, 3, 5, 2, 6, 1, 7)
     x_far = (2, 1, 3)
     row_far = (8, 9, 7, 10, 6, 11, 5, 12, 4, 13, 3, 14, 2, 15, 1)
@@ -141,7 +137,7 @@
     for d in range(16):
         ct[d] = ucf[pl.ds(d, 128, stride=16), :].astype(BF16)
     cr[0] = ct[0]
-    for d in (13, 4, 12, 5, 11, 6, 10, 7, 9, 8):
+    for d in (3, 13, 4, 12, 5, 11, 6, 10, 7, 9, 8, 1, 15, 2, 14):
         push(ct.at[d], cr.at[d], 7, at_row(d))
     load_u0.wait()
     for d in x_far:
@@ -168,8 +164,6 @@
     for dx, dy in col_far:
         push(p3s.at[lax.rem(xx + dx, XS)], p3.at[col], 6, at_col(dx, dy))
     p3[col] = p3s[xx]
-    for d in (1, 15, 2, 14, 3):
-        push(ct.at[d], cr.at[d], 7, at_row(d))
     whole(sg.at[pl.ds(1, 3)], 3).wait_recv()
     below0 = jnp.concatenate([sg[j][:, :64] for j in range(XS)], axis=1)
     y0 = jnp.concatenate([sg[j][:, 64:] for j in range(XS)], axis=1)
@@ -205,6 +199,20 @@
     for d in x_far:
         push(w0s, w0g.at[d], 10, at_x(d))
 
+    whole(xfull.at[1, pl.ds(0, 24)], 9).wait_recv()
+    x1 = xfull[1]
+    x_out[:, 1, :] = x1
+    xb[1] = x1.astype(BF16)
+    total = jnp.zeros((32, 128), F32)
+    for d in range(16):
+        slot = d * 16 + lax.rem(row - d + 16, 16)
+        term = dot(xb[cmap[child, slot] // ROWS], cr[d], NT)
+        total += jnp.where(slot < cnt[child], term, 0.0)
+    p6s[...] = total.reshape(4, 8, 128)
+    for d in x_far:
+        push(p6s.at[lax.rem(xx + d, XS)], p6.at[d], 12, at_x(d))
+    p6[0] = p6s[xx]
+
     whole(p4.at[pl.ds(0, 15)], 8).wait_recv()
     s0 = p4[0].astype(F32)
     for k in range(1, ROWS):
@@ -216,32 +224,16 @@
     for d in y_far:
         push(p5s, p5.at[yy], 11, at_y(d))
 
-    whole(xfull.at[1, pl.ds(0, 24)], 9).wait_recv()
-    x1 = xfull[1]
-    x_out[:, 1, :] = x1
-    xb[1] = x1.astype(BF16)
-    total = jnp.zeros((32, 128), F32)
-    for d in range(16):
-        slot = d * 16 + lax.rem(row - d + 16, 16)
-        term = dot(xb[cmap[child, slot] // ROWS], cr[d], NT)
-        total += jnp.where(slot < cnt[child], term, 0.0)
-    p6a[...] = total
-    push(p6a, p6r, 12, sibling)
     whole(w0g.at[pl.ds(1, 3)], 10).wait_recv()
-    whole(p6r, 12).wait_recv()
-    chip = (p6a[...] + p6r[...]).astype(BF16)
-    p6s[...] = chip
-    p6z[z] = chip
-    for d in z_far:
-        push(p6s, p6z.at[z], 13, at_z(d))
+    whole(p6.at[pl.ds(1, 3)], 12).wait_recv()
 
     whole(p5.at[pl.ds(0, 7)], 11).wait_recv()
     x0 = p5[0]
     for k in range(1, YS):
         x0 += p5[k]
-    late = dot(x0.astype(BF16), w0g[...].reshape(512, 128), NT).astype(BF16)
+    late = dot(x0.astype(BF16), w0g[...].reshape(512, 128), NT)
     for j in range(XS):
-        p7s[j] = late[:, 128 * j:128 * j + 128]
+        p7s[j] = (p6[j] + late[:, 128 * j:128 * j + 128]).astype(BF16)
     for dr, dx in row_x_far:
         push(p7s.at[(XS - dx) % XS], p7.at[xx * ROWS + row], 14, at_row_x(dr, dx))
     p7[xx * ROWS + row] = p7s[0]
@@ -249,6 +241,17 @@
     for d in x_far:
         push(xfull.at[0, mine], xfull.at[0, mine], 15, at_x(d))
 
+    whole(xfull.at[0, pl.ds(0, 24)], 15).wait()
+    x_out[:, 0, :] = xfull[0]
+    save_x = load(x_out, x_hbm, 10)
+
+    whole(p7.at[pl.ds(0, 63)], 14).wait()
+    for j in range(XS):
+        late = p7[j * ROWS].astype(F32)
+        for k in range(1, ROWS):
+            late += p7[j * ROWS + k].astype(F32)
+        c_out[pl.ds(8 * j, 8), :] = rc[pl.ds(8 * j, 8), :] - late
+    save_c = load(c_out, c_hbm, 11)
     whole(p1r.at[pl.ds(0, 15)], 0).wait_send()
     whole(sg.at[pl.ds(1, 3)], 3).wait_send()
     whole(l10g.at[pl.ds(1, 3)], 4).wait_send()
@@ -259,23 +262,10 @@
     whole(xfull.at[1, pl.ds(0, 24)], 9).wait_send()
     whole(w0g.at[pl.ds(1, 3)], 10).wait_send()
     whole(p5.at[pl.ds(0, 7)], 11).wait_send()
-    whole(p6r, 12).wait_send()
-    whole(p6z.at[pl.ds(0, 7)], 13).wait_send()
-
-    whole(p6z.at[pl.ds(0, 7)], 13).wait_recv()
-    total = p6z[0].astype(F32)
-    for k in range(1, ZS):
-        total += p6z[k].astype(F32)
-    total = rc[...] - total
-    whole(xfull.at[0, pl.ds(0, 24)], 15).wait()
-    x_out[:, 0, :] = xfull[0]
-
-    whole(p7.at[pl.ds(0, 63)], 14).wait()
-    for j in range(XS):
-        late = p7[j * ROWS].astype(F32)
-        for k in range(1, ROWS):
-            late += p7[j * ROWS + k].astype(F32)
-        c_out[pl.ds(8 * j, 8), :] = total[8 * j:8 * j + 8] - late
+    whole(p6.at[pl.ds(1, 3)], 12).wait_send()
+
+    save_x.wait()
+    save_c.wait()
 
 
 def local(
@@ -300,7 +290,7 @@
             jax.ShapeDtypeStruct((32, 128), F32),
         ),
         in_specs=[pl.BlockSpec(memory_space=pl.ANY)] * 9,
-        out_specs=(pl.BlockSpec(memory_space=vm), pl.BlockSpec(memory_space=vm)),
+        out_specs=(pl.BlockSpec(memory_space=pl.ANY), pl.BlockSpec(memory_space=pl.ANY)),
         scratch_shapes=[
             vm((2, 25, 64, 128), BF16),
             vm((2, 64, 128), BF16),
@@ -329,13 +319,13 @@
             vm((16, 16, 128), BF16),
             vm((8, 128), F32),
             vm((8, 8, 128), F32),
-            vm((32, 128), F32),
-            vm((32, 128), F32),
-            vm((32, 128), BF16),
-            vm((8, 32, 128), BF16),
+            vm((4, 8, 128), F32),
+            vm((4, 8, 128), F32),
             vm((4, 8, 128), BF16),
             vm((64, 8, 128), BF16),
-            pltpu.SemaphoreType.DMA((10,)),
+            vm((32, 2, 128), F32),
+            vm((32, 128), F32),
+            pltpu.SemaphoreType.DMA((12,)),
             pltpu.SemaphoreType.DMA((16,)),
             pltpu.SemaphoreType.DMA((16,)),
             pltpu.SemaphoreType.REGULAR,

time: 47.5 us -> 47.4 us (level)
  no operation moved by 1% of the time
where the time goes in v5:
time: 47.4 us; the launch traced here: 47.2 us
  Pallas kernels  44.6 us (94%)
  local copies, waits for them, and re-layouts  1.99 us (4%)
  between operations  0.65 us (1%)
    pallas_call x1, Pallas kernels, local(): pl.pallas_call(kernel, out_shape=(jax.ShapeDtypeStruct((32, 2, 128), F32)...  44.6 us
    unnamed x4, local copies, waits for them, and re-layouts  1.99 us

profile of v5, /device:TPU:1, one launch (start us, length us, event | category | flops | bytes accessed | tf_op | source)
XLA Modules:
  0.0 47.2 jit_solution(11438678551229598057)
XLA Ops:
  0.6 44.6 %solve.1 = (f32[32,2,128]{2,1,0:T(2,128)}, f32[32,128]{1,0:T(8,128)}) custom-call(bf16[2,25,64,128]{3,2,1,0:T(8,128)(2,1)} %bitcast.3, bf16[2,64,128]{2,1,0:T(8,128)(2,1)} %bitcast.5, f32[32,2,64]{2,1,0:T(2,128)} %rhs_hbm.1, f32[2,64]{1,0:T(2,128)} %piv_hbm.1, bf16[23,32,128]{2,1,0:T(8,128)(2,1)} %bitcast.4, bf16[128,16,128]{2,1,0:T(8,128)(2,1)} %uc_hbm.1, ...), custom_call_target="tpu_custom_call" | custom-call | tf_op jit(solution)/shard_map/solve/pallas_call | solution.py:286
  45.2 0.0 copy-start
  45.2 1.4 %copy.13 = f32[32,2,128]{2,1,0:T(2,128)} copy(f32[32,2,128]{2,1,0:T(2,128)} %get-tuple-element.4) | data formatting | bytes 65536
  46.6 0.0 copy-done
  46.6 0.6 %copy.14 = f32[32,128]{1,0:T(8,128)} copy(f32[32,128]{1,0:T(8,128)S(1)} %copy-done) | data formatting | bytes 32768
Async XLA Ops:
  45.2 1.4 %copy-start = (f32[32,128]{1,0:T(8,128)S(1)}, f32[32,128]{1,0:T(8,128)}, u32[]{:S(2)}) copy-start(f32[32,128]{1,0:T(8,128)} %get-tuple-element.5) | copy-start | bytes 49156

commit v6 on v5

--- a/solution.py
+++ b/solution.py
@@ -137,7 +137,7 @@
     for d in range(16):
         ct[d] = ucf[pl.ds(d, 128, stride=16), :].astype(BF16)
     cr[0] = ct[0]
-    for d in (3, 13, 4, 12, 5, 11, 6, 10, 7, 9, 8, 1, 15, 2, 14):
+    for d in (5, 11, 6, 10, 7, 9, 8):
         push(ct.at[d], cr.at[d], 7, at_row(d))
     load_u0.wait()
     for d in x_far:
@@ -164,6 +164,8 @@
     for dx, dy in col_far:
         push(p3s.at[lax.rem(xx + dx, XS)], p3.at[col], 6, at_col(dx, dy))
     p3[col] = p3s[xx]
+    for d in (1, 15, 2, 14, 3, 13, 4, 12):
+        push(ct.at[d], cr.at[d], 7, at_row(d))
     whole(sg.at[pl.ds(1, 3)], 3).wait_recv()
     below0 = jnp.concatenate([sg[j][:, :64] for j in range(XS)], axis=1)
     y0 = jnp.concatenate([sg[j][:, 64:] for j in range(XS)], axis=1)

time: 47.4 us -> 47.4 us (level)
  no operation moved by 1% of the time
where the time goes in v6:
time: 47.4 us; the launch traced here: 47.2 us
  Pallas kernels  44.6 us (94%)
  local copies, waits for them, and re-layouts  1.99 us (4%)
  between operations  0.65 us (1%)
    pallas_call x1, Pallas kernels, local(): pl.pallas_call(kernel, out_shape=(jax.ShapeDtypeStruct((32, 2, 128), F32)...  44.6 us
    unnamed x4, local copies, waits for them, and re-layouts  1.99 us

profile of v6, /device:TPU:1, one launch (start us, length us, event | category | flops | bytes accessed | tf_op | source)
XLA Modules:
  0.0 47.2 jit_solution(16481759859435241093)
XLA Ops:
  0.6 44.6 %solve.1 = (f32[32,2,128]{2,1,0:T(2,128)}, f32[32,128]{1,0:T(8,128)}) custom-call(bf16[2,25,64,128]{3,2,1,0:T(8,128)(2,1)} %bitcast.3, bf16[2,64,128]{2,1,0:T(8,128)(2,1)} %bitcast.5, f32[32,2,64]{2,1,0:T(2,128)} %rhs_hbm.1, f32[2,64]{1,0:T(2,128)} %piv_hbm.1, bf16[23,32,128]{2,1,0:T(8,128)(2,1)} %bitcast.4, bf16[128,16,128]{2,1,0:T(8,128)(2,1)} %uc_hbm.1, ...), custom_call_target="tpu_custom_call" | custom-call | tf_op jit(solution)/shard_map/solve/pallas_call | solution.py:288
  45.2 0.0 copy-start
  45.2 1.4 %copy.13 = f32[32,2,128]{2,1,0:T(2,128)} copy(f32[32,2,128]{2,1,0:T(2,128)} %get-tuple-element.4) | data formatting | bytes 65536
  46.6 0.0 copy-done
  46.6 0.6 %copy.14 = f32[32,128]{1,0:T(8,128)} copy(f32[32,128]{1,0:T(8,128)S(1)} %copy-done) | data formatting | bytes 32768
Async XLA Ops:
  45.2 1.4 %copy-start = (f32[32,128]{1,0:T(8,128)S(1)}, f32[32,128]{1,0:T(8,128)}, u32[]{:S(2)}) copy-start(f32[32,128]{1,0:T(8,128)} %get-tuple-element.5) | copy-start | bytes 49156
